TPU v7x, 32 devices: a whole 2x2x4 slice. The times are simulated.
32 devices in a mesh: parts: 2 (over x), seq: 8 (over z, y), dp: 2 (over core).
Axes of the slice: x: 2, y: 2, z: 4, core: 2. Of those that a mesh axis runs over, the one named last changes fastest.
Arguments:
- activations: bfloat16 [8, 2048, 1024], P(('parts', 'dp'), 'seq'), parts along dimension 0, may hold values from -36 to 36, as said below
- cotangent: bfloat16 [8, 2048, 1024], P(('parts', 'dp'), 'seq'), parts along dimension 0, may hold values from -6 to 6
- conv_one: bfloat16 [1024, 3, 512], P(('seq', 'dp')), may hold values from -0.109375 to 0.109375
- mix_one: bfloat16 [512, 1024], P(('seq', 'dp')), may hold values from -0.25 to 0.25
- conv_two: bfloat16 [1024, 3, 512], P(('seq', 'dp')), may hold values from -0.109375 to 0.109375
- mix_two: bfloat16 [512, 1024], P(('seq', 'dp')), may hold values from -0.25 to 0.25
Outputs:
- input_grad: bfloat16 [8, 2048, 1024], P(('parts', 'dp'), 'seq'), parts along dimension 0
- grad_conv_one: float32 [2048, 3, 512], P(('parts', 'seq', 'dp')), parts along dimension 0
- grad_mix_one: float32 [1024, 1024], P(('parts', 'seq', 'dp')), parts along dimension 0
- grad_conv_two: float32 [2048, 3, 512], P(('parts', 'seq', 'dp')), parts along dimension 0
- grad_mix_two: float32 [1024, 1024], P(('parts', 'seq', 'dp')), parts along dimension 0
There are 2 independent parts, one for each index of `parts`. A program takes and returns all parts, laid end to end along the dimension named above; an argument that names none is the same for every part. Nothing has to cross between parts.
Inputs may be any that keep to these rules, and one draw needn't show every extreme that they name: activations of earlier layers.
All inputs are finite; a program needn't handle non-finite values.
Results may differ from a plain program's by a relative error of at most 0.007.
Values may be sent and summed in bfloat16 or wider, within the bound.
No kernel may reach another device: no remote copies, remote signals or barrier semaphores. Data moves between devices by JAX's collectives and lax.ppermute only.
A program may use at most 128 MiB of HBM per device.

v0:
```python
import jax
import jax.numpy as jnp
from jax import lax
from jax.sharding import PartitionSpec as P

DILATE_ONE = 64
DILATE_TWO = 128


def with_halo(block, sides, width):
    for axis, dim in sides:
        count = lax.axis_size(axis)
        forward = [(i, i + 1) for i in range(count - 1)]
        backward = [(target, source) for source, target in forward]
        low = lax.ppermute(
            lax.slice_in_dim(block, block.shape[dim] - width, None, axis=dim), axis, forward
        )
        high = lax.ppermute(lax.slice_in_dim(block, 0, width, axis=dim), axis, backward)
        block = jnp.concatenate([low, block, high], axis=dim)
    return block


def prenorm(values):
    scale = lax.rsqrt(jnp.mean(values * values, axis=-1, keepdims=True) + 1e-06)
    return jax.nn.gelu(values * scale)


def fetch(conv_w, mix_w):
    return (
        lax.all_gather(conv_w, ("seq", "dp"), axis=0, tiled=True),
        lax.all_gather(mix_w, ("seq", "dp"), axis=0, tiled=True),
    )


def extended(field, dilate):
    return with_halo(field, (("seq", 1),), dilate)


def views_of(padded, dilate, length):
    return [padded[:, tap * dilate : tap * dilate + length] for tap in range(3)]


def forward(inputs, full_conv, full_mix, dilate):
    width = inputs.shape[-1]
    length = inputs.shape[1]
    normed = prenorm(inputs.astype(jnp.float32)).astype(jnp.bfloat16)
    views = views_of(extended(normed, dilate), dilate, length)
    flat_views = [view.reshape(-1, width) for view in views]
    preact = jnp.dot(flat_views[0], full_conv[:, 0, :], preferred_element_type=jnp.float32)
    for tap in range(1, 3):
        preact = preact + jnp.dot(
            flat_views[tap], full_conv[:, tap, :], preferred_element_type=jnp.float32
        )
    hidden = jax.nn.gelu(preact).astype(jnp.bfloat16)
    mixed = inputs.reshape(-1, width).astype(jnp.float32) + jnp.dot(
        hidden, full_mix, preferred_element_type=jnp.float32
    )
    return (mixed.astype(jnp.bfloat16).reshape(inputs.shape), flat_views, preact, hidden)


def backward(
    inputs, flat_views, preact, hidden, upstream, full_conv, full_mix, conv_rows, mix_rows, dilate
):
    width = inputs.shape[-1]
    length = inputs.shape[1]
    middle = full_mix.shape[0]
    flat_up = upstream.reshape(-1, width)
    contract = (((0,), (0,)), ((), ()))
    dhidden = jnp.dot(flat_up, full_mix.T, preferred_element_type=jnp.float32)
    unused, pull = jax.vjp(jax.nn.gelu, preact)
    dpre = pull(dhidden)[0].astype(jnp.bfloat16)
    piece = hidden
    grad_mix = lax.psum_scatter(
        lax.dot_general(piece, flat_up, contract, preferred_element_type=jnp.float32),
        ("seq", "dp"),
        scatter_dimension=0,
        tiled=True,
    )
    terms = []
    for conv_tap in range(3):
        piece = flat_views[conv_tap]
        terms.append(lax.dot_general(piece, dpre, contract, preferred_element_type=jnp.float32))
    grad_conv = lax.psum_scatter(
        jnp.stack(terms, axis=1), ("seq", "dp"), scatter_dimension=0, tiled=True
    )
    dpre_field = dpre.reshape(inputs.shape[0], length, middle)
    back_views = views_of(extended(dpre_field, dilate), dilate, length)
    dnormed = jnp.dot(
        back_views[2].reshape(-1, middle), full_conv[:, 0, :].T, preferred_element_type=jnp.float32
    )
    for tap in range(1, 3):
        dnormed = dnormed + jnp.dot(
            back_views[2 - tap].reshape(-1, middle),
            full_conv[:, tap, :].T,
            preferred_element_type=jnp.float32,
        )
    unused_two, pull_norm = jax.vjp(prenorm, inputs.astype(jnp.float32))
    dinput = pull_norm(dnormed.reshape(inputs.shape))[0]
    result = (upstream.astype(jnp.float32) + dinput).astype(jnp.bfloat16)
    return (result, grad_conv, grad_mix)


def body(activations, cotangent, conv_one, mix_one, conv_two, mix_two):
    conv_full_one, mix_full_one = fetch(conv_one, mix_one)
    second_in, views_one, preact_one, hidden_one = forward(
        activations, conv_full_one, mix_full_one, DILATE_ONE
    )
    conv_full_two, mix_full_two = fetch(conv_two, mix_two)
    unused, views_two, preact_two, hidden_two = forward(
        second_in, conv_full_two, mix_full_two, DILATE_TWO
    )
    conv_back_two, mix_back_two = (conv_full_two, mix_full_two)
    upstream, grad_conv_two, grad_mix_two = backward(
        second_in,
        views_two,
        preact_two,
        hidden_two,
        cotangent,
        conv_back_two,
        mix_back_two,
        conv_two.shape[0],
        mix_two.shape[0],
        DILATE_TWO,
    )
    conv_back_one, mix_back_one = (conv_full_one, mix_full_one)
    input_grad, grad_conv_one, grad_mix_one = backward(
        activations,
        views_one,
        preact_one,
        hidden_one,
        upstream,
        conv_back_one,
        mix_back_one,
        conv_one.shape[0],
        mix_one.shape[0],
        DILATE_ONE,
    )
    return (input_grad, grad_conv_one, grad_mix_one, grad_conv_two, grad_mix_two)


def solution(mesh):
    in_specs = (
        P(("parts", "dp"), "seq", None),
        P(("parts", "dp"), "seq", None),
        P(("seq", "dp"), None, None),
        P(("seq", "dp"), None),
        P(("seq", "dp"), None, None),
        P(("seq", "dp"), None),
    )
    out_specs = (
        P(("parts", "dp"), "seq", None),
        P(("parts", "seq", "dp"), None, None),
        P(("parts", "seq", "dp"), None),
        P(("parts", "seq", "dp"), None, None),
        P(("parts", "seq", "dp"), None),
    )
    return jax.shard_map(body, mesh=mesh, in_specs=in_specs, out_specs=out_specs, check_vma=False)
```

profile of v0, /device:TPU:0, one launch (start us, length us, event | category | flops | bytes accessed | tf_op | source)
XLA Modules:
  0.0 512.4 jit_solution(3078574404284320583)
XLA Ops:
  12.4 4.9 collective-permute-start
  18.6 12.0 %collective-permute-done = bf16[2,64,1024]{2,1,0:T(8,128)(2,1)S(1)} collective-permute-done((bf16[2,64,1024]{2,1,0:T(8,128)(2,1)S(1)}, bf16[2,64,1024]{2,1,0:T(8,128)(2,1)S(1)}, u32[]{:S(2)}, u32[]{:S(2)}) %collective-permute-start) | collective-permute-done | bytes 262176 | tf_op jit(solution)/shard_map/ppermute | solution.py:15
  31.9 31.0 %all-gather.7.cloned.1.call-done = bf16[1024,3,512]{2,0,1:T(8,128)(2,1)} async-done(((bf16[64,3,512]{2,0,1:T(8,128)(2,1)}), bf16[1024,3,512]{2,0,1:T(8,128)(2,1)}) %all-gather.7.cloned.1.call-update) | async-done | bytes 3145744 | tf_op jit(solution)/shard_map/all_gather | solution.py:30
  62.9 2.1 fusion.60
  67.0 34.9 %all-gather.9.cloned.1.call-done = bf16[512,1024]{1,0:T(8,128)(2,1)} async-done(((bf16[32,1024]{1,0:T(8,128)(2,1)}), bf16[512,1024]{1,0:T(8,128)(2,1)}) %all-gather.9.cloned.1.call-update) | async-done | bytes 1048592 | tf_op jit(solution)/shard_map/all_gather | solution.py:31
  101.8 3.1 fusion.36
  105.0 3.4 fusion.39
  110.4 3.2 collective-permute-start.2
  114.9 28.7 %all-gather.5.cloned.1.call-done = bf16[512,1024]{1,0:T(8,128)(2,1)} async-done(((bf16[32,1024]{1,0:T(8,128)(2,1)}), bf16[512,1024]{1,0:T(8,128)(2,1)}) %all-gather.5.cloned.1.call-update) | async-done | bytes 1048592 | tf_op jit(solution)/shard_map/all_gather | solution.py:31
  143.6 2.9 fusion.84
  146.5 43.3 %all-gather.11.cloned.1.call-done = bf16[1024,3,512]{2,0,1:T(8,128)(2,1)} async-done(((bf16[64,3,512]{2,0,1:T(8,128)(2,1)}), bf16[1024,3,512]{2,0,1:T(8,128)(2,1)}) %all-gather.11.cloned.1.call-update) | async-done | bytes 3145744 | tf_op jit(solution)/shard_map/all_gather | solution.py:30
  189.9 2.6 fusion.63
  197.6 2.2 fusion.66
  199.9 2.5 collective-permute-start.5
  204.2 2.0 fusion.62
  206.1 2.2 collective-permute-done.5
  208.4 5.5 %collective-permute-done.4 = bf16[2,128,512]{2,1,0:T(8,128)(2,1)S(1)} collective-permute-done((bf16[2,128,512]{2,1,0:T(8,128)(2,1)S(1)}, bf16[2,128,512]{2,1,0:T(8,128)(2,1)S(1)}, u32[]{:S(2)}, u32[]{:S(2)}) %collective-permute-start.4) | collective-permute-done | bytes 262176 | tf_op jit(solution)/shard_map/ppermute | solution.py:18
  215.1 3.3 fusion.20
  218.5 3.8 fusion.22
  223.3 2.2 fusion.77
  225.6 2.2 convolution_bitcast_fusion
  230.3 3.4 pad_maximum_fusion.1
  233.8 3.2 fusion.48
  239.7 3.4 pad_maximum_fusion
  243.1 4.4 collective-permute-start.7
  249.3 2.0 fusion.57
  251.3 5.5 %collective-permute-done.6 = bf16[2,64,512]{2,1,0:T(8,128)(2,1)S(1)} collective-permute-done((bf16[2,64,512]{2,1,0:T(8,128)(2,1)S(1)}, bf16[2,64,512]{2,1,0:T(8,128)(2,1)S(1)}, u32[]{:S(2)}, u32[]{:S(2)}) %collective-permute-start.6) | collective-permute-done | bytes 131104 | tf_op jit(solution)/shard_map/ppermute | solution.py:18
  258.3 1.9 fusion.32
  260.3 3.0 fusion.24
  263.3 63.9 %reduce-scatter.7.cloned.1.call-done = f32[32,1024]{1,0:T(8,128)} async-done(((f32[512,1024]{1,0:T(8,128)}), f32[32,1024]{1,0:T(8,128)}) %reduce-scatter.7.cloned.1.call-update) | async-done | bytes 131088 | tf_op jit(solution)/shard_map/reduce_scatter | solution.py:73
  327.2 88.8 %reduce-scatter.9.cloned.1.call-done = f32[64,3,512]{2,0,1:T(8,128)} async-done(((f32[1024,3,512]{2,0,1:T(8,128)}), f32[64,3,512]{2,0,1:T(8,128)}) %reduce-scatter.9.cloned.1.call-update) | async-done | bytes 393232 | tf_op jit(solution)/shard_map/reduce_scatter | solution.py:83
  416.0 89.6 %reduce-scatter.5.cloned.1.call-done = f32[64,3,512]{2,0,1:T(8,128)} async-done(((f32[1024,3,512]{2,0,1:T(8,128)}), f32[64,3,512]{2,0,1:T(8,128)}) %reduce-scatter.5.cloned.1.call-update) | async-done | bytes 393232 | tf_op jit(solution)/shard_map/reduce_scatter | solution.py:83
  (100 shorter events, 30.9 us)
Async XLA Ops:
  7.2 4.4 copy-start
  7.2 55.7 %all-gather.7.cloned.1.call-start = ((), (), s32[]{:S(2)}) async-start(), calls=%async_computation.5 | async-start | bytes 3342336 | tf_op jit(solution)/shard_map/all_gather | solution.py:30
  7.9 93.9 %all-gather.9.cloned.1.call-start = ((), (), s32[]{:S(2)}) async-start(), calls=%async_computation.6 | async-start | bytes 1114112 | tf_op jit(solution)/shard_map/all_gather | solution.py:31
  8.7 134.9 %all-gather.5.cloned.1.call-start = ((), (), s32[]{:S(2)}) async-start(), calls=%async_computation.4 | async-start | bytes 1114112 | tf_op jit(solution)/shard_map/all_gather | solution.py:31
  9.4 180.5 %all-gather.11.cloned.1.call-start = ((), (), s32[]{:S(2)}) async-start(), calls=%async_computation.7 | async-start | bytes 3342336 | tf_op jit(solution)/shard_map/all_gather | solution.py:30
  10.0 253.3 %reduce-scatter.11.cloned.1.call-start = ((), (), s32[]{:S(2)}) async-start(), calls=%async_computation.11 | async-start | bytes 2228224 | tf_op jit(solution)/shard_map/reduce_scatter | solution.py:73
  12.4 18.2 %collective-permute-start = (bf16[2,64,1024]{2,1,0:T(8,128)(2,1)S(1)}, bf16[2,64,1024]{2,1,0:T(8,128)(2,1)S(1)}, u32[]{:S(2)}, u32[]{:S(2)}) collective-permute-start(bf16[2,64,1024]{2,1,0:T(8,128)(2,1)S(1)} %get-tuple-element.13), channel_id=1, source_target_pairs={{0,2},{2,4},{4,6},{6,8},{8,10},{10,12},{12,14},{1,3},{3,5},{5,7},{... | collective-permute-start | bytes 786440 | tf_op jit(solution)/shard_map/ppermute | solution.py:15
  17.3 13.3 %collective-permute-start.1 = (bf16[2,64,1024]{2,1,0:T(8,128)(2,1)S(1)}, bf16[2,64,1024]{2,1,0:T(8,128)(2,1)S(1)}, u32[]{:S(2)}, u32[]{:S(2)}) collective-permute-start(bf16[2,64,1024]{2,1,0:T(8,128)(2,1)S(1)} %get-tuple-element.14), channel_id=1, source_target_pairs={{2,0},{4,2},{6,4},{8,6},{10,8},{12,10},{14,12},{3,1},{5,3},{7,5},{... | collective-permute-start | bytes 786440 | tf_op jit(solution)/shard_map/ppermute | solution.py:18
  31.9 34.0 %copy-start.7 = (bf16[2,256,1024]{2,1,0:T(8,128)(2,1)}, bf16[2,256,1024]{2,1,0:T(8,128)(2,1)S(1)}, u32[]{:S(2)}) copy-start(bf16[2,256,1024]{2,1,0:T(8,128)(2,1)S(1)} %get-tuple-element.12) | copy-start | bytes 3145732
  62.9 2.2 copy-start.5
  66.9 38.0 %copy-start.16 = (f32[512,512]{1,0:T(8,128)}, f32[512,512]{1,0:T(8,128)S(1)}, u32[]{:S(2)}) copy-start(f32[512,512]{1,0:T(8,128)S(1)} %fusion.41) | copy-start | bytes 3145732
  108.3 35.3 %copy-start.18 = (bf16[2,256,1024]{2,1,0:T(8,128)(2,1)S(1)}, bf16[2,256,1024]{2,1,0:T(8,128)(2,1)}, u32[]{:S(2)}) copy-start(bf16[2,256,1024]{2,1,0:T(8,128)(2,1)} %param.7) | copy-start | bytes 3145732
  110.4 82.1 %collective-permute-start.2 = (bf16[2,128,1024]{2,1,0:T(8,128)(2,1)}, bf16[2,128,1024]{2,1,0:T(8,128)(2,1)}, u32[]{:S(2)}, u32[]{:S(2)}) collective-permute-start(bf16[2,128,1024]{2,1,0:T(8,128)(2,1)} %get-tuple-element.9), channel_id=1, source_target_pairs={{0,2},{2,4},{4,6},{6,8},{8,10},{10,12},{12,14},{1,3},{3,5},{5,7},{... | collective-permute-start | bytes 1572872 | tf_op jit(solution)/shard_map/ppermute | solution.py:15
  113.6 78.9 %collective-permute-start.3 = (bf16[2,128,1024]{2,1,0:T(8,128)(2,1)}, bf16[2,128,1024]{2,1,0:T(8,128)(2,1)}, u32[]{:S(2)}, u32[]{:S(2)}) collective-permute-start(bf16[2,128,1024]{2,1,0:T(8,128)(2,1)} %get-tuple-element.10), channel_id=1, source_target_pairs={{2,0},{4,2},{6,4},{8,6},{10,8},{12,10},{14,12},{3,1},{5,3},{7,5},{... | collective-permute-start | bytes 1572872 | tf_op jit(solution)/shard_map/ppermute | solution.py:18
  189.9 2.7 copy-start.4
  192.5 2.2 copy-start.14
  194.1 3.5 copy-start.9
  194.1 3.5 copy-start.11
  194.1 2.1 copy-start.22
  199.8 127.3 %reduce-scatter.7.cloned.1.call-start = ((), (), s32[]{:S(2)}) async-start(), calls=%async_computation.9 | async-start | bytes 2228224 | tf_op jit(solution)/shard_map/reduce_scatter | solution.py:73
  199.9 8.4 %collective-permute-start.5 = (bf16[2,128,512]{2,1,0:T(8,128)(2,1)S(1)}, bf16[2,128,512]{2,1,0:T(8,128)(2,1)S(1)}, u32[]{:S(2)}, u32[]{:S(2)}) collective-permute-start(bf16[2,128,512]{2,1,0:T(8,128)(2,1)S(1)} %get-tuple-element.21), channel_id=1, source_target_pairs={{0,2},{2,4},{4,6},{6,8},{8,10},{10,12},{12,14},{1,3},{3,5},{5,7},{... | collective-permute-start | bytes 786440 | tf_op jit(solution)/shard_map/ppermute | solution.py:15
  202.4 11.5 %copy-start.15 = (bf16[1024,3,512]{2,0,1:T(8,128)(2,1)S(1)}, bf16[1024,3,512]{2,0,1:T(8,128)(2,1)}, u32[]{:S(2)}) copy-start(bf16[1024,3,512]{2,0,1:T(8,128)(2,1)} %all-gather.11.cloned.1.call-done) | copy-start | bytes 9437188
  202.4 11.4 %collective-permute-start.4 = (bf16[2,128,512]{2,1,0:T(8,128)(2,1)S(1)}, bf16[2,128,512]{2,1,0:T(8,128)(2,1)S(1)}, u32[]{:S(2)}, u32[]{:S(2)}) collective-permute-start(bf16[2,128,512]{2,1,0:T(8,128)(2,1)S(1)} %get-tuple-element.22), channel_id=1, source_target_pairs={{2,0},{4,2},{6,4},{8,6},{10,8},{12,10},{14,12},{3,1},{5,3},{7,5},{... | collective-permute-start | bytes 786440 | tf_op jit(solution)/shard_map/ppermute | solution.py:18
  218.5 4.8 copy-start.17
  225.5 190.5 %reduce-scatter.9.cloned.1.call-start = ((), (), s32[]{:S(2)}) async-start(), calls=%async_computation.10 | async-start | bytes 6684672 | tf_op jit(solution)/shard_map/reduce_scatter | solution.py:83
  225.6 2.3 copy-start.10
  233.7 271.9 %reduce-scatter.5.cloned.1.call-start = ((), (), s32[]{:S(2)}) async-start(), calls=%async_computation.8 | async-start | bytes 6684672 | tf_op jit(solution)/shard_map/reduce_scatter | solution.py:83
  233.8 3.2 copy-start.8
  243.1 8.1 %collective-permute-start.7 = (bf16[2,64,512]{2,1,0:T(8,128)(2,1)S(1)}, bf16[2,64,512]{2,1,0:T(8,128)(2,1)S(1)}, u32[]{:S(2)}, u32[]{:S(2)}) collective-permute-start(bf16[2,64,512]{2,1,0:T(8,128)(2,1)S(1)} %get-tuple-element.17), channel_id=1, source_target_pairs={{0,2},{2,4},{4,6},{6,8},{8,10},{10,12},{12,14},{1,3},{3,5},{5,7},{... | collective-permute-start | bytes 393224 | tf_op jit(solution)/shard_map/ppermute | solution.py:15
  247.5 9.3 %copy-start.6 = (bf16[1024,3,512]{2,0,1:T(8,128)(2,1)S(1)}, bf16[1024,3,512]{2,0,1:T(8,128)(2,1)}, u32[]{:S(2)}) copy-start(bf16[1024,3,512]{2,0,1:T(8,128)(2,1)} %all-gather.7.cloned.1.call-done) | copy-start | bytes 9437188
  247.5 9.2 %collective-permute-start.6 = (bf16[2,64,512]{2,1,0:T(8,128)(2,1)S(1)}, bf16[2,64,512]{2,1,0:T(8,128)(2,1)S(1)}, u32[]{:S(2)}, u32[]{:S(2)}) collective-permute-start(bf16[2,64,512]{2,1,0:T(8,128)(2,1)S(1)} %get-tuple-element.18), channel_id=1, source_target_pairs={{2,0},{4,2},{6,4},{8,6},{10,8},{12,10},{14,12},{3,1},{5,3},{7,5},{... | collective-permute-start | bytes 393224 | tf_op jit(solution)/shard_map/ppermute | solution.py:18
  258.3 1.9 copy-start.13
  (7 other events, 8.4 us)
Sparse Core Ops, SparseCore 0:
  10.2 52.6 all-gather.6
  65.0 36.7 all-gather.8
  104.0 39.5 all-gather.4
  145.6 44.1 all-gather.10
  199.9 62.3 reduce-scatter.10
  266.9 60.1 reduce-scatter.6
  331.7 84.2 reduce-scatter.8
  421.0 84.4 reduce-scatter.4
where the time goes:
time: 513 us; the launch traced here: 512 us
  waiting for transfers between devices  408 us (80%)
  matrix products  37.7 us (7%)
  other arithmetic  24.2 us (5%)
  starting transfers between devices  21.4 us (4%)
  between operations  14.6 us (3%)
  local copies, waits for them, and re-layouts  6.65 us (1%)
    reduce_scatter x2, waiting for transfers between devices, backward(): lax.psum_scatter(jnp.stack(terms, axis=1), ('seq', 'dp'), scatter_dimensi...  178 us
    all_gather x2, waiting for transfers between devices, fetch(): lax.all_gather(conv_w, ('seq', 'dp'), axis=0, tiled=True)  74.3 us
    reduce_scatter x2, waiting for transfers between devices, backward(): lax.psum_scatter(lax.dot_general(piece, flat_up, contract, preferred_elem...  63.9 us
    all_gather x2, waiting for transfers between devices, fetch(): lax.all_gather(mix_w, ('seq', 'dp'), axis=0, tiled=True)  63.6 us
    ppermute x4, starting transfers between devices, with_halo(): lax.ppermute(lax.slice_in_dim(block, block.shape[dim] - width, None, axis...  15 us
    ppermute x4, waiting for transfers between devices, with_halo(): lax.ppermute(lax.slice_in_dim(block, block.shape[dim] - width, None, axis...  14.2 us
    ppermute x4, waiting for transfers between devices, with_halo(): lax.ppermute(lax.slice_in_dim(block, 0, width, axis=dim), axis, backward)  10.9 us
  transfers between devices with their start and end apart: 16, of which 11 were waited for; matrix products, arithmetic and copies ran while one was open for 11% of the time, Pallas kernels for 0%

commit v1 on v0

--- a/solution.py
+++ b/solution.py
@@ -5,6 +5,19 @@
 
 DILATE_ONE = 64
 DILATE_TWO = 128
+
+
+def ring_gather(x, axis, dim):
+    ways = lax.axis_size(axis)
+    up = [(d, (d + 1) % ways) for d in range(ways)]
+    down = [(d, (d - 1) % ways) for d in range(ways)]
+    earlier, later = ([x], [x])
+    for _ in range(ways // 2):
+        earlier.append(lax.ppermute(earlier[-1], axis, up))
+    for _ in range((ways - 1) // 2):
+        later.append(lax.ppermute(later[-1], axis, down))
+    line = jnp.concatenate([*earlier[::-1], *later[1:]], axis=dim)
+    return jnp.roll(line, (lax.axis_index(axis) - ways // 2) * x.shape[dim], axis=dim)
 
 
 def with_halo(block, sides, width):
@@ -28,7 +41,7 @@
 def fetch(conv_w, mix_w):
     return (
         lax.all_gather(conv_w, ("seq", "dp"), axis=0, tiled=True),
-        lax.all_gather(mix_w, ("seq", "dp"), axis=0, tiled=True),
+        ring_gather(mix_w, ("seq", "dp"), 0),
     )
 
 

time: 513 us -> 458 us (0.89)
  waiting for transfers between devices: 408 us -> 275 us
  starting transfers between devices: 21.4 us -> 75.1 us
  local copies, waits for them, and re-layouts: 6.65 us -> 32 us
    all_gather x2, waiting for transfers between devices: 74.3 us -> 0.01 us  [fetch(): lax.all_gather(conv_w, ('seq', 'dp'), axis=0, tiled=True)]
    all_gather x2 -> x0, waiting for transfers between devices: 63.6 us -> none  [fetch(): lax.all_gather(mix_w, ('seq', 'dp'), axis=0, tiled=True)]
    ppermute x0 -> x30, starting transfers between devices: none -> 56.9 us  [the longest x14 47.9 us: ring_gather(): later.append(lax.ppermute(later[-1], axis, down))]
    unnamed x46 -> x100, local copies, waits for them, and re-layouts: 5.46 us -> 28.6 us
    ppermute x4, waiting for transfers between devices: 14.2 us -> 23.5 us  [with_halo(): lax.ppermute(lax.slice_in_dim(block, block.shape[dim] - width, None, axis...]
    ppermute x4, waiting for transfers between devices: 10.9 us -> 3.59 us  [with_halo(): lax.ppermute(lax.slice_in_dim(block, 0, width, axis=dim), axis, backward)]
    ppermute x0 -> x30, waiting for transfers between devices: none -> 6.94 us  [the longest x16 6.37 us: ring_gather(): earlier.append(lax.ppermute(earlier[-1], axis, up))]
  transfers between devices with their start and end apart: 16 -> 44, of which waited for: 11 -> 14; matrix products, arithmetic and copies ran while one was open for 11% -> 18% of each run, Pallas kernels for 0% -> 0%
where the time goes in v1:
time: 458 us; the launch traced here: 457 us
  waiting for transfers between devices  275 us (60%)
  starting transfers between devices  75.1 us (16%)
  matrix products  35.8 us (8%)
  local copies, waits for them, and re-layouts  32 us (7%)
  other arithmetic  24.2 us (5%)
  between operations  14.8 us (3%)
    reduce_scatter x2, waiting for transfers between devices, backward(): lax.psum_scatter(jnp.stack(terms, axis=1), ('seq', 'dp'), scatter_dimensi...  178 us
    reduce_scatter x2, waiting for transfers between devices, backward(): lax.psum_scatter(lax.dot_general(piece, flat_up, contract, preferred_elem...  62 us
    ppermute x14, starting transfers between devices, ring_gather(): later.append(lax.ppermute(later[-1], axis, down))  47.9 us
    unnamed x100, local copies, waits for them, and re-layouts  28.6 us
    ppermute x4, waiting for transfers between devices, with_halo(): lax.ppermute(lax.slice_in_dim(block, block.shape[dim] - width, None, axis...  23.5 us
    ppermute x4, starting transfers between devices, with_halo(): lax.ppermute(lax.slice_in_dim(block, block.shape[dim] - width, None, axis...  12.2 us
  transfers between devices with their start and end apart: 44, of which 14 were waited for; matrix products, arithmetic and copies ran while one was open for 18% of the time, Pallas kernels for 0%

profile of v1, /device:TPU:0, one launch (start us, length us, event | category | flops | bytes accessed | tf_op | source)
XLA Modules:
  0.0 456.6 jit_solution(3405056509146850486)
XLA Ops:
  8.4 5.1 %collective-permute-start.25 = (bf16[32,1024]{1,0:T(8,128)(2,1)}, bf16[32,1024]{1,0:T(8,128)(2,1)S(1)}, u32[]{:S(2)}, u32[]{:S(2)}) collective-permute-start(bf16[32,1024]{1,0:T(8,128)(2,1)} %param.11), channel_id=1, source_target_pairs={{0,15},{1,0},{2,1},{3,2},{4,3},{5,4},{6,5},{7,6},{8,7},{9,8},{10,9... | collective-permute-start | bytes 196616 | tf_op jit(solution)/shard_map/ppermute | solution.py:18
  13.5 4.4 collective-permute-start.8
  21.7 4.4 collective-permute-start.26
  27.5 4.4 collective-permute-start.9
  32.0 4.4 collective-permute-start.27
  36.4 4.4 collective-permute-start.10
  42.8 3.9 collective-permute-start.28
  48.9 4.6 %collective-permute-start.11 = (bf16[32,1024]{1,0:T(8,128)(2,1)S(1)}, bf16[32,1024]{1,0:T(8,128)(2,1)S(1)}, u32[]{:S(2)}, u32[]{:S(2)}) collective-permute-start(bf16[32,1024]{1,0:T(8,128)(2,1)S(1)} %collective-permute-done.10), channel_id=1, source_target_pairs={{0,15},{1,0},{2,1},{3,2},{4,3},{5,4},{6,5},{7,6},{8,7},{9,8},{10,9... | collective-permute-start | bytes 196616 | tf_op jit(solution)/shard_map/ppermute | solution.py:18
  54.1 5.6 %collective-permute-start.4 = (bf16[32,1024]{1,0:T(8,128)(2,1)S(1)}, bf16[32,1024]{1,0:T(8,128)(2,1)S(1)}, u32[]{:S(2)}, u32[]{:S(2)}) collective-permute-start(bf16[32,1024]{1,0:T(8,128)(2,1)S(1)} %collective-permute-done.3), channel_id=1, source_target_pairs={{0,1},{1,2},{2,3},{3,4},{4,5},{5,6},{6,7},{7,8},{8,9},{9,10},{10,1... | collective-permute-start | bytes 196616 | tf_op jit(solution)/shard_map/ppermute | solution.py:16
  61.4 2.8 collective-permute-start.29
  66.6 4.5 collective-permute-start.30
  74.3 4.4 collective-permute-start.31
  106.5 2.9 fusion.36
  109.5 2.2 fusion.39
  120.2 2.3 fusion.68
  122.6 15.2 %collective-permute-done.32 = bf16[2,128,1024]{2,1,0:T(8,128)(2,1)} collective-permute-done((bf16[2,128,1024]{2,1,0:T(8,128)(2,1)}, bf16[2,128,1024]{2,1,0:T(8,128)(2,1)}, u32[]{:S(2)}, u32[]{:S(2)}) %collective-permute-start.32) | collective-permute-done | bytes 524320 | tf_op jit(solution)/shard_map/ppermute | solution.py:28
  141.8 2.2 fusion.71
  144.0 3.4 fusion.55
  147.5 4.4 collective-permute-start.35
  153.9 8.3 %collective-permute-done.35 = bf16[2,128,512]{2,1,0:T(8,128)(2,1)S(1)} collective-permute-done((bf16[2,128,512]{2,1,0:T(8,128)(2,1)S(1)}, bf16[2,128,512]{2,1,0:T(8,128)(2,1)S(1)}, u32[]{:S(2)}, u32[]{:S(2)}) %collective-permute-start.35) | collective-permute-done | bytes 262176 | tf_op jit(solution)/shard_map/ppermute | solution.py:28
  163.5 3.3 fusion.20
  166.9 3.8 fusion.22
  171.7 2.2 fusion.84
  178.4 3.3 pad_maximum_fusion.1
  182.1 3.4 fusion.48
  188.2 3.4 pad_maximum_fusion
  191.7 4.4 collective-permute-start.37
  199.6 3.6 collective-permute-done.36
  206.7 3.0 fusion.24
  209.7 62.0 %reduce-scatter.7.cloned.1.call-done = f32[32,1024]{1,0:T(8,128)} async-done(((f32[512,1024]{1,0:T(8,128)}), f32[32,1024]{1,0:T(8,128)}) %reduce-scatter.7.cloned.1.call-update) | async-done | bytes 131088 | tf_op jit(solution)/shard_map/reduce_scatter | solution.py:86
  271.8 88.7 %reduce-scatter.9.cloned.1.call-done = f32[64,3,512]{2,0,1:T(8,128)} async-done(((f32[1024,3,512]{2,0,1:T(8,128)}), f32[64,3,512]{2,0,1:T(8,128)}) %reduce-scatter.9.cloned.1.call-update) | async-done | bytes 393232 | tf_op jit(solution)/shard_map/reduce_scatter | solution.py:96
  360.4 89.3 %reduce-scatter.5.cloned.1.call-done = f32[64,3,512]{2,0,1:T(8,128)} async-done(((f32[1024,3,512]{2,0,1:T(8,128)}), f32[64,3,512]{2,0,1:T(8,128)}) %reduce-scatter.5.cloned.1.call-update) | async-done | bytes 393232 | tf_op jit(solution)/shard_map/reduce_scatter | solution.py:96
  (210 shorter events, 77.5 us)
Async XLA Ops:
  7.2 94.8 %all-gather.3.cloned.1.call-start = ((), (), s32[]{:S(2)}) async-start(), calls=%async_computation.4 | async-start | bytes 3342336 | tf_op jit(solution)/shard_map/all_gather | solution.py:43
  7.9 112.3 %all-gather.5.cloned.1.call-start = ((), (), s32[]{:S(2)}) async-start(), calls=%async_computation.5 | async-start | bytes 3342336 | tf_op jit(solution)/shard_map/all_gather | solution.py:43
  7.9 13.6 %collective-permute-start.17 = (bf16[32,1024]{1,0:T(8,128)(2,1)}, bf16[32,1024]{1,0:T(8,128)(2,1)S(1)}, u32[]{:S(2)}, u32[]{:S(2)}) collective-permute-start(bf16[32,1024]{1,0:T(8,128)(2,1)} %param.11), channel_id=1, source_target_pairs={{0,1},{1,2},{2,3},{3,4},{4,5},{5,6},{6,7},{7,8},{8,9},{9,10},{10,1... | collective-permute-start | bytes 196616 | tf_op jit(solution)/shard_map/ppermute | solution.py:16
  8.4 13.2 %collective-permute-start.25 = (bf16[32,1024]{1,0:T(8,128)(2,1)}, bf16[32,1024]{1,0:T(8,128)(2,1)S(1)}, u32[]{:S(2)}, u32[]{:S(2)}) collective-permute-start(bf16[32,1024]{1,0:T(8,128)(2,1)} %param.11), channel_id=1, source_target_pairs={{0,15},{1,0},{2,1},{3,2},{4,3},{5,4},{6,5},{7,6},{8,7},{9,8},{10,9... | collective-permute-start | bytes 196616 | tf_op jit(solution)/shard_map/ppermute | solution.py:18
  13.5 13.9 %collective-permute-start = (bf16[32,1024]{1,0:T(8,128)(2,1)}, bf16[32,1024]{1,0:T(8,128)(2,1)S(1)}, u32[]{:S(2)}, u32[]{:S(2)}) collective-permute-start(bf16[32,1024]{1,0:T(8,128)(2,1)} %param.13), channel_id=1, source_target_pairs={{0,1},{1,2},{2,3},{3,4},{4,5},{5,6},{6,7},{7,8},{8,9},{9,10},{10,1... | collective-permute-start | bytes 196616 | tf_op jit(solution)/shard_map/ppermute | solution.py:16
  13.5 14.0 %collective-permute-start.8 = (bf16[32,1024]{1,0:T(8,128)(2,1)}, bf16[32,1024]{1,0:T(8,128)(2,1)S(1)}, u32[]{:S(2)}, u32[]{:S(2)}) collective-permute-start(bf16[32,1024]{1,0:T(8,128)(2,1)} %param.13), channel_id=1, source_target_pairs={{0,15},{1,0},{2,1},{3,2},{4,3},{5,4},{6,5},{7,6},{8,7},{9,8},{10,9... | collective-permute-start | bytes 196616 | tf_op jit(solution)/shard_map/ppermute | solution.py:18
  21.6 10.4 %collective-permute-start.18 = (bf16[32,1024]{1,0:T(8,128)(2,1)S(1)}, bf16[32,1024]{1,0:T(8,128)(2,1)S(1)}, u32[]{:S(2)}, u32[]{:S(2)}) collective-permute-start(bf16[32,1024]{1,0:T(8,128)(2,1)S(1)} %collective-permute-done.17), channel_id=1, source_target_pairs={{0,1},{1,2},{2,3},{3,4},{4,5},{5,6},{6,7},{7,8},{8,9},{9,10},{10,1... | collective-permute-start | bytes 196616 | tf_op jit(solution)/shard_map/ppermute | solution.py:16
  21.7 10.3 %collective-permute-start.26 = (bf16[32,1024]{1,0:T(8,128)(2,1)S(1)}, bf16[32,1024]{1,0:T(8,128)(2,1)S(1)}, u32[]{:S(2)}, u32[]{:S(2)}) collective-permute-start(bf16[32,1024]{1,0:T(8,128)(2,1)S(1)} %collective-permute-done.25), channel_id=1, source_target_pairs={{0,15},{1,0},{2,1},{3,2},{4,3},{5,4},{6,5},{7,6},{8,7},{9,8},{10,9... | collective-permute-start | bytes 196616 | tf_op jit(solution)/shard_map/ppermute | solution.py:18
  26.1 35.3 %collective-permute-start.15 = (bf16[2,64,1024]{2,1,0:T(8,128)(2,1)S(1)}, bf16[2,64,1024]{2,1,0:T(8,128)(2,1)S(1)}, u32[]{:S(2)}, u32[]{:S(2)}) collective-permute-start(bf16[2,64,1024]{2,1,0:T(8,128)(2,1)S(1)} %get-tuple-element.14), channel_id=1, source_target_pairs={{0,2},{2,4},{4,6},{6,8},{8,10},{10,12},{12,14},{1,3},{3,5},{5,7},{... | collective-permute-start | bytes 786440 | tf_op jit(solution)/shard_map/ppermute | solution.py:28
  27.4 9.0 %collective-permute-start.1 = (bf16[32,1024]{1,0:T(8,128)(2,1)S(1)}, bf16[32,1024]{1,0:T(8,128)(2,1)S(1)}, u32[]{:S(2)}, u32[]{:S(2)}) collective-permute-start(bf16[32,1024]{1,0:T(8,128)(2,1)S(1)} %collective-permute-done), channel_id=1, source_target_pairs={{0,1},{1,2},{2,3},{3,4},{4,5},{5,6},{6,7},{7,8},{8,9},{9,10},{10,1... | collective-permute-start | bytes 196616 | tf_op jit(solution)/shard_map/ppermute | solution.py:16
  27.5 8.9 %collective-permute-start.9 = (bf16[32,1024]{1,0:T(8,128)(2,1)S(1)}, bf16[32,1024]{1,0:T(8,128)(2,1)S(1)}, u32[]{:S(2)}, u32[]{:S(2)}) collective-permute-start(bf16[32,1024]{1,0:T(8,128)(2,1)S(1)} %collective-permute-done.8), channel_id=1, source_target_pairs={{0,15},{1,0},{2,1},{3,2},{4,3},{5,4},{6,5},{7,6},{8,7},{9,8},{10,9... | collective-permute-start | bytes 196616 | tf_op jit(solution)/shard_map/ppermute | solution.py:18
  31.9 8.9 %collective-permute-start.19 = (bf16[32,1024]{1,0:T(8,128)(2,1)S(1)}, bf16[32,1024]{1,0:T(8,128)(2,1)S(1)}, u32[]{:S(2)}, u32[]{:S(2)}) collective-permute-start(bf16[32,1024]{1,0:T(8,128)(2,1)S(1)} %collective-permute-done.18), channel_id=1, source_target_pairs={{0,1},{1,2},{2,3},{3,4},{4,5},{5,6},{6,7},{7,8},{8,9},{9,10},{10,1... | collective-permute-start | bytes 196616 | tf_op jit(solution)/shard_map/ppermute | solution.py:16
  32.0 8.9 %collective-permute-start.27 = (bf16[32,1024]{1,0:T(8,128)(2,1)S(1)}, bf16[32,1024]{1,0:T(8,128)(2,1)S(1)}, u32[]{:S(2)}, u32[]{:S(2)}) collective-permute-start(bf16[32,1024]{1,0:T(8,128)(2,1)S(1)} %collective-permute-done.26), channel_id=1, source_target_pairs={{0,15},{1,0},{2,1},{3,2},{4,3},{5,4},{6,5},{7,6},{8,7},{9,8},{10,9... | collective-permute-start | bytes 196616 | tf_op jit(solution)/shard_map/ppermute | solution.py:18
  36.4 10.3 %collective-permute-start.10 = (bf16[32,1024]{1,0:T(8,128)(2,1)S(1)}, bf16[32,1024]{1,0:T(8,128)(2,1)S(1)}, u32[]{:S(2)}, u32[]{:S(2)}) collective-permute-start(bf16[32,1024]{1,0:T(8,128)(2,1)S(1)} %collective-permute-done.9), channel_id=1, source_target_pairs={{0,15},{1,0},{2,1},{3,2},{4,3},{5,4},{6,5},{7,6},{8,7},{9,8},{10,9... | collective-permute-start | bytes 196616 | tf_op jit(solution)/shard_map/ppermute | solution.py:18
  40.9 7.5 %collective-permute-start.20 = (bf16[32,1024]{1,0:T(8,128)(2,1)S(1)}, bf16[32,1024]{1,0:T(8,128)(2,1)S(1)}, u32[]{:S(2)}, u32[]{:S(2)}) collective-permute-start(bf16[32,1024]{1,0:T(8,128)(2,1)S(1)} %collective-permute-done.19), channel_id=1, source_target_pairs={{0,1},{1,2},{2,3},{3,4},{4,5},{5,6},{6,7},{7,8},{8,9},{9,10},{10,1... | collective-permute-start | bytes 196616 | tf_op jit(solution)/shard_map/ppermute | solution.py:16
  40.9 32.1 %collective-permute-start.16 = (bf16[2,64,1024]{2,1,0:T(8,128)(2,1)S(1)}, bf16[2,64,1024]{2,1,0:T(8,128)(2,1)S(1)}, u32[]{:S(2)}, u32[]{:S(2)}) collective-permute-start(bf16[2,64,1024]{2,1,0:T(8,128)(2,1)S(1)} %get-tuple-element.15), channel_id=1, source_target_pairs={{2,0},{4,2},{6,4},{8,6},{10,8},{12,10},{14,12},{3,1},{5,3},{7,5},{... | collective-permute-start | bytes 786440 | tf_op jit(solution)/shard_map/ppermute | solution.py:31
  48.3 11.4 %collective-permute-start.21 = (bf16[32,1024]{1,0:T(8,128)(2,1)S(1)}, bf16[32,1024]{1,0:T(8,128)(2,1)S(1)}, u32[]{:S(2)}, u32[]{:S(2)}) collective-permute-start(bf16[32,1024]{1,0:T(8,128)(2,1)S(1)} %collective-permute-done.20), channel_id=1, source_target_pairs={{0,1},{1,2},{2,3},{3,4},{4,5},{5,6},{6,7},{7,8},{8,9},{9,10},{10,1... | collective-permute-start | bytes 196616 | tf_op jit(solution)/shard_map/ppermute | solution.py:16
  48.9 15.3 %collective-permute-start.11 = (bf16[32,1024]{1,0:T(8,128)(2,1)S(1)}, bf16[32,1024]{1,0:T(8,128)(2,1)S(1)}, u32[]{:S(2)}, u32[]{:S(2)}) collective-permute-start(bf16[32,1024]{1,0:T(8,128)(2,1)S(1)} %collective-permute-done.10), channel_id=1, source_target_pairs={{0,15},{1,0},{2,1},{3,2},{4,3},{5,4},{6,5},{7,6},{8,7},{9,8},{10,9... | collective-permute-start | bytes 196616 | tf_op jit(solution)/shard_map/ppermute | solution.py:18
  54.1 10.1 %collective-permute-start.4 = (bf16[32,1024]{1,0:T(8,128)(2,1)S(1)}, bf16[32,1024]{1,0:T(8,128)(2,1)S(1)}, u32[]{:S(2)}, u32[]{:S(2)}) collective-permute-start(bf16[32,1024]{1,0:T(8,128)(2,1)S(1)} %collective-permute-done.3), channel_id=1, source_target_pairs={{0,1},{1,2},{2,3},{3,4},{4,5},{5,6},{6,7},{7,8},{8,9},{9,10},{10,1... | collective-permute-start | bytes 196616 | tf_op jit(solution)/shard_map/ppermute | solution.py:16
  66.5 143.3 %reduce-scatter.11.cloned.1.call-start = ((), (), s32[]{:S(2)}) async-start(), calls=%async_computation.9 | async-start | bytes 2228224 | tf_op jit(solution)/shard_map/reduce_scatter | solution.py:86
  66.6 7.8 %collective-permute-start.30 = (bf16[32,1024]{1,0:T(8,128)(2,1)}, bf16[32,1024]{1,0:T(8,128)(2,1)S(1)}, u32[]{:S(2)}, u32[]{:S(2)}) collective-permute-start(bf16[32,1024]{1,0:T(8,128)(2,1)} %collective-permute-done.29), channel_id=1, source_target_pairs={{0,15},{1,0},{2,1},{3,2},{4,3},{5,4},{6,5},{7,6},{8,7},{9,8},{10,9... | collective-permute-start | bytes 196616 | tf_op jit(solution)/shard_map/ppermute | solution.py:18
  71.1 7.7 %collective-permute-start.13 = (bf16[32,1024]{1,0:T(8,128)(2,1)}, bf16[32,1024]{1,0:T(8,128)(2,1)}, u32[]{:S(2)}, u32[]{:S(2)}) collective-permute-start(bf16[32,1024]{1,0:T(8,128)(2,1)} %collective-permute-done.12), channel_id=1, source_target_pairs={{0,15},{1,0},{2,1},{3,2},{4,3},{5,4},{6,5},{7,6},{8,7},{9,8},{10,9... | collective-permute-start | bytes 196616 | tf_op jit(solution)/shard_map/ppermute | solution.py:18
  74.3 26.9 %collective-permute-start.31 = (bf16[32,1024]{1,0:T(8,128)(2,1)S(1)}, bf16[32,1024]{1,0:T(8,128)(2,1)S(1)}, u32[]{:S(2)}, u32[]{:S(2)}) collective-permute-start(bf16[32,1024]{1,0:T(8,128)(2,1)S(1)} %collective-permute-done.30), channel_id=1, source_target_pairs={{0,15},{1,0},{2,1},{3,2},{4,3},{5,4},{6,5},{7,6},{8,7},{9,8},{10,9... | collective-permute-start | bytes 196616 | tf_op jit(solution)/shard_map/ppermute | solution.py:18
  78.8 40.0 %collective-permute-start.14 = (bf16[32,1024]{1,0:T(8,128)(2,1)}, bf16[32,1024]{1,0:T(8,128)(2,1)}, u32[]{:S(2)}, u32[]{:S(2)}) collective-permute-start(bf16[32,1024]{1,0:T(8,128)(2,1)} %collective-permute-done.13), channel_id=1, source_target_pairs={{0,15},{1,0},{2,1},{3,2},{4,3},{5,4},{6,5},{7,6},{8,7},{9,8},{10,9... | collective-permute-start | bytes 196616 | tf_op jit(solution)/shard_map/ppermute | solution.py:18
  113.8 24.0 %collective-permute-start.32 = (bf16[2,128,1024]{2,1,0:T(8,128)(2,1)}, bf16[2,128,1024]{2,1,0:T(8,128)(2,1)}, u32[]{:S(2)}, u32[]{:S(2)}) collective-permute-start(bf16[2,128,1024]{2,1,0:T(8,128)(2,1)} %get-tuple-element.10), channel_id=1, source_target_pairs={{0,2},{2,4},{4,6},{6,8},{8,10},{10,12},{12,14},{1,3},{3,5},{5,7},{... | collective-permute-start | bytes 1572872 | tf_op jit(solution)/shard_map/ppermute | solution.py:28
  115.8 22.0 %collective-permute-start.33 = (bf16[2,128,1024]{2,1,0:T(8,128)(2,1)}, bf16[2,128,1024]{2,1,0:T(8,128)(2,1)}, u32[]{:S(2)}, u32[]{:S(2)}) collective-permute-start(bf16[2,128,1024]{2,1,0:T(8,128)(2,1)} %get-tuple-element.11), channel_id=1, source_target_pairs={{2,0},{4,2},{6,4},{8,6},{10,8},{12,10},{14,12},{3,1},{5,3},{7,5},{... | collective-permute-start | bytes 1572872 | tf_op jit(solution)/shard_map/ppermute | solution.py:31
  144.0 127.8 %reduce-scatter.7.cloned.1.call-start = ((), (), s32[]{:S(2)}) async-start(), calls=%async_computation.7 | async-start | bytes 2228224 | tf_op jit(solution)/shard_map/reduce_scatter | solution.py:86
  147.5 14.7 %collective-permute-start.35 = (bf16[2,128,512]{2,1,0:T(8,128)(2,1)S(1)}, bf16[2,128,512]{2,1,0:T(8,128)(2,1)S(1)}, u32[]{:S(2)}, u32[]{:S(2)}) collective-permute-start(bf16[2,128,512]{2,1,0:T(8,128)(2,1)S(1)} %get-tuple-element.22), channel_id=1, source_target_pairs={{0,2},{2,4},{4,6},{6,8},{8,10},{10,12},{12,14},{1,3},{3,5},{5,7},{... | collective-permute-start | bytes 786440 | tf_op jit(solution)/shard_map/ppermute | solution.py:28
  151.9 10.3 %collective-permute-start.34 = (bf16[2,128,512]{2,1,0:T(8,128)(2,1)S(1)}, bf16[2,128,512]{2,1,0:T(8,128)(2,1)S(1)}, u32[]{:S(2)}, u32[]{:S(2)}) collective-permute-start(bf16[2,128,512]{2,1,0:T(8,128)(2,1)S(1)} %get-tuple-element.23), channel_id=1, source_target_pairs={{2,0},{4,2},{6,4},{8,6},{10,8},{12,10},{14,12},{3,1},{5,3},{7,5},{... | collective-permute-start | bytes 786440 | tf_op jit(solution)/shard_map/ppermute | solution.py:31
  173.9 186.5 %reduce-scatter.9.cloned.1.call-start = ((), (), s32[]{:S(2)}) async-start(), calls=%async_computation.8 | async-start | bytes 6684672 | tf_op jit(solution)/shard_map/reduce_scatter | solution.py:96
  181.8 267.9 %reduce-scatter.5.cloned.1.call-start = ((), (), s32[]{:S(2)}) async-start(), calls=%async_computation.6 | async-start | bytes 6684672 | tf_op jit(solution)/shard_map/reduce_scatter | solution.py:96
  191.7 7.9 %collective-permute-start.37 = (bf16[2,64,512]{2,1,0:T(8,128)(2,1)S(1)}, bf16[2,64,512]{2,1,0:T(8,128)(2,1)S(1)}, u32[]{:S(2)}, u32[]{:S(2)}) collective-permute-start(bf16[2,64,512]{2,1,0:T(8,128)(2,1)S(1)} %get-tuple-element.18), channel_id=1, source_target_pairs={{0,2},{2,4},{4,6},{6,8},{8,10},{10,12},{12,14},{1,3},{3,5},{5,7},{... | collective-permute-start | bytes 393224 | tf_op jit(solution)/shard_map/ppermute | solution.py:28
  (47 other events, 380.5 us)
Sparse Core Ops, SparseCore 0:
  10.2 58.8 all-gather.2
  71.3 44.7 all-gather.4
  144.1 62.0 reduce-scatter.10
  210.8 60.8 reduce-scatter.6
  276.1 84.2 reduce-scatter.8
  365.3 84.3 reduce-scatter.4
